TPU v7x, 32 devices: a whole 2x2x4 slice. The times are simulated.
32 devices in a mesh: lon: 8 (over z, y), lat: 4 (over x, core).
Axes of the slice: x: 2, y: 2, z: 4, core: 2. Of those that a mesh axis runs over, the one named last changes fastest.
Arguments:
- ocean_state: float32 [4, 8, 64, 1024], P(None, None, 'lat', 'lon'), may hold values from -5 to 5
- thickness: float32 [8, 64, 1024], P(None, 'lat', 'lon'), may hold values from 0.5 to 2
- wet_mask: int32 [8, 64, 1024], P(None, 'lat', 'lon'), may hold values 0 or 1
- mode_counts: int32 [64], P('lat'), may hold values from 1 to 64, as said below
- row_flags: int32 [64], P('lat'), may hold values from 0 to 1, as said below
Outputs:
- ocean_next: float32 [4, 8, 64, 1024], P(None, None, 'lat', 'lon')
Inputs may be any that keep to these rules, and one draw needn't show every extreme that they name: `mode_counts`: mode counts lie in the range; row 0 keeps 64. `row_flags`: only rows among the first 16 or the last 16 are flagged; the first and the last row always are.
All inputs are finite; a program needn't handle non-finite values. No bound on the sum of `wet_mask` on one device may be relied on, other than what follows from the above.
Results may differ from a plain program's by a relative error of at most 0.0003.
Values sent between devices are 32-bit elements; how exact they have to be, the bound alone decides.
No kernel may reach another device: no remote copies, remote signals or barrier semaphores. Data moves between devices by JAX's collectives and lax.ppermute only.
A program may use at most 64 MiB of HBM per device.

v0:
```python
import math
import jax
import jax.numpy as jnp
from jax import lax
from jax.sharding import PartitionSpec as P

FBAND = 16
MAXM = 64
lat_edge = 1.3
diffusion = 0.05
vertical_mix = 0.5
time_step = 0.05


def with_halo(array, sides, width, wrap):
    for axis, dim in sides:
        peers, length = (lax.axis_size(axis), array.shape[dim])
        up = [(i, (i + 1) % peers) for i in range(peers if wrap else peers - 1)]
        down = [(j, i) for i, j in up]
        last = lax.slice_in_dim(array, length - width, length, axis=dim)
        leading = lax.slice_in_dim(array, 0, width, axis=dim)
        before = lax.ppermute(last, axis, up)
        after = lax.ppermute(leading, axis, down)
        array = jnp.concatenate([before, array, after], axis=dim)
    return array


def advance(padded, u_pad, v_pad, static, centre, faces):
    thick = static[0]
    wet = static[1]
    inv_c = 1.0 / centre
    east_u = 0.5 * (u_pad[:, :, :-1] + u_pad[:, :, 1:])
    east_h = 0.5 * (thick[:, :, :-1] + thick[:, :, 1:]) * wet[:, :, :-1] * wet[:, :, 1:]
    flux_e = east_h[None] * (
        east_u[None] * 0.5 * (padded[..., :-1] + padded[..., 1:])
        - diffusion * (padded[..., 1:] - padded[..., :-1]) * inv_c[:, None]
    )
    zonal = (flux_e[..., 1:] - flux_e[..., :-1])[:, :, 1:-1, :] * inv_c[1:-1, None]
    north_v = 0.5 * (v_pad[:, :-1, :] + v_pad[:, 1:, :])
    north_h = (
        0.5 * (thick[:, :-1, :] + thick[:, 1:, :]) * wet[:, :-1, :] * wet[:, 1:, :] * faces[:, None]
    )
    flux_n = north_h[None] * (
        north_v[None] * 0.5 * (padded[:, :, :-1] + padded[:, :, 1:])
        - diffusion * (padded[:, :, 1:] - padded[:, :, :-1])
    )
    merid = (flux_n[:, :, 1:] - flux_n[:, :, :-1])[..., 1:-1] * inv_c[1:-1, None]
    inner = padded[:, :, 1:-1, 1:-1]
    wet_in = wet[:, 1:-1, 1:-1]
    thick_in = jnp.where(wet_in > 0, thick[:, 1:-1, 1:-1], 1.0)
    coupling = wet_in[:-1] * wet_in[1:] * vertical_mix / (0.5 * (thick_in[:-1] + thick_in[1:]))
    vmix = coupling[None] * (inner[:, 1:] - inner[:, :-1])
    empty = jnp.zeros_like(vmix[:, :1])
    vert = jnp.concatenate([vmix, empty], axis=1) - jnp.concatenate([empty, vmix], axis=1)
    return inner + wet_in[None] * time_step * (vert - zonal - merid) / thick_in[None]


def mode_basis(index, length, modes):
    turns = jnp.arange(modes, dtype=jnp.int32)[None, :] * index[:, None] % length
    angle = turns.astype(jnp.float32) * (2.0 * math.pi / length)
    return jnp.concatenate([jnp.cos(angle), jnp.sin(angle)], axis=1)


def mode_weights(counts, modes, length):
    order = jnp.arange(modes).astype(jnp.float32)
    keep = (order[None, :] < counts[:, None]).astype(jnp.float32)
    scale = jnp.where(order == 0, 1.0, 2.0) / length
    weights = keep * scale[None, :]
    return jnp.concatenate([weights, weights], axis=1)


def extend(fields, width):
    wider = with_halo(fields, (("lon", 3),), width, True)
    return with_halo(wider, (("lat", 2),), width, False)


def shards(ocean_state, thickness, wet_mask, mode_counts, row_flags):
    wet = wet_mask.astype(jnp.float32)
    static = jnp.stack([thickness, wet])
    levels = ocean_state.shape[1]
    rows = ocean_state.shape[2]
    lanes = ocean_state.shape[3]
    nlat = rows * lax.axis_size("lat")
    nlon = lanes * lax.axis_size("lon")
    lat_pos = lax.axis_index("lat")
    lon_pos = lax.axis_index("lon")
    joined = extend(jnp.concatenate([ocean_state, static], axis=0), 1)
    fields = joined[:4]
    fixed = joined[4:]
    index = lat_pos * rows - 1 + jnp.arange(rows + 2 * 1, dtype=jnp.int32)
    place = index.astype(jnp.float32)
    centre = jnp.cos(lat_edge * (2.0 * (place + 0.5) / nlat - 1.0))
    faces = jnp.cos(lat_edge * (2.0 * (place[:-1] + 1.0) / nlat - 1.0))
    centre, faces = (centre, faces)
    state = advance(fields, fields[2], fields[3], fixed, centre, faces)
    fields = extend(state, 1)
    state = advance(fields, fields[2], fields[3], fixed, centre, faces)
    flags = row_flags.astype(jnp.float32)
    counts = mode_counts.astype(jnp.float32)
    total = 4 * levels * FBAND
    flat = state.reshape(total, lanes)
    row_counts = jnp.broadcast_to(counts[None, None, :], (4, levels, FBAND)).reshape(total)
    index = lon_pos * lanes + jnp.arange(lanes, dtype=jnp.int32)
    basis = mode_basis(index, nlon, MAXM)
    partial_sum = jnp.dot(
        flat, basis, precision=lax.Precision.HIGHEST, preferred_element_type=jnp.float32
    )
    totals = lax.psum(partial_sum, "lon")
    smooth = jnp.dot(
        totals * mode_weights(row_counts, MAXM, nlon),
        basis.T,
        precision=lax.Precision.HIGHEST,
        preferred_element_type=jnp.float32,
    )
    smooth = smooth.reshape(4, levels, FBAND, lanes)
    filtered = state + flags[None, None, :, None] * wet[None] * (smooth - state)
    return filtered


def solution(mesh):
    in_specs = (
        P(None, None, "lat", "lon"),
        P(None, "lat", "lon"),
        P(None, "lat", "lon"),
        P("lat"),
        P("lat"),
    )
    out_specs = P(None, None, "lat", "lon")
    return jax.shard_map(shards, mesh=mesh, in_specs=in_specs, out_specs=out_specs, check_vma=False)
```

profile of v0, /device:TPU:0, one launch (start us, length us, event | category | flops | bytes accessed | tf_op | source)
XLA Modules:
  0.0 145.7 jit_solution(13678122371583939406)
XLA Ops:
  6.5 0.8 convert_bitcast_fusion
  7.4 1.1 pad_maximum_fusion.13
  8.7 6.1 %collective-permute-start.1 = (f32[6,8,16,1]{3,2,1,0:T(8,128)S(1)}, f32[6,8,16,1]{3,2,1,0:T(8,128)S(1)}, u32[]{:S(2)}, u32[]{:S(2)}) collective-permute-start(f32[6,8,16,1]{3,2,1,0:T(8,128)S(1)} %get-tuple-element.24), channel_id=1, source_target_pairs={{4,0},{8,4},{12,8},{16,12},{20,16},{24,20},{28,24},{0,28},{5,1},{9... | collective-permute-start | bytes 9224 | tf_op jit(solution)/shard_map/ppermute | solution.py:23
  14.8 0.3 fusion.35
  15.3 13.9 %collective-permute-done.1 = f32[6,8,16,1]{3,2,1,0:T(8,128)S(1)} collective-permute-done((f32[6,8,16,1]{3,2,1,0:T(8,128)S(1)}, f32[6,8,16,1]{3,2,1,0:T(8,128)S(1)}, u32[]{:S(2)}, u32[]{:S(2)}) %collective-permute-start.1) | collective-permute-done | bytes 3104 | tf_op jit(solution)/shard_map/ppermute | solution.py:23
  29.4 0.4 pad_maximum_fusion.15
  29.8 1.9 %collective-permute-start.2 = (f32[6,8,1,130]{3,2,1,0:T(1,128)S(1)}, f32[6,8,1,130]{3,2,1,0:T(1,128)S(1)}, u32[]{:S(2)}, u32[]{:S(2)}) collective-permute-start(f32[6,8,1,130]{3,2,1,0:T(1,128)S(1)} %get-tuple-element.10), channel_id=1, source_target_pairs={{0,1},{1,2},{2,3},{4,5},{5,6},{6,7},{8,9},{9,10},{10,11},{12,13},{... | collective-permute-start | bytes 74888 | tf_op jit(solution)/shard_map/ppermute | solution.py:22
  31.7 1.3 collective-permute-start.3
  33.1 2.9 %collective-permute-done.3 = f32[6,8,1,130]{3,2,1,0:T(1,128)S(1)} collective-permute-done((f32[6,8,1,130]{3,2,1,0:T(1,128)S(1)}, f32[6,8,1,130]{3,2,1,0:T(1,128)S(1)}, u32[]{:S(2)}, u32[]{:S(2)}) %collective-permute-start.3) | collective-permute-done | bytes 24992 | tf_op jit(solution)/shard_map/ppermute | solution.py:23
  36.0 0.5 pad_maximum_fusion
  36.8 0.6 subtract_multiply_fusion.2
  37.8 0.3 subtract_multiply_fusion.3
  38.8 4.8 %collective-permute-start.5 = (f32[4,8,16,1]{3,2,1,0:T(8,128)S(1)}, f32[4,8,16,1]{3,2,1,0:T(8,128)S(1)}, u32[]{:S(2)}, u32[]{:S(2)}) collective-permute-start(f32[4,8,16,1]{3,2,1,0:T(8,128)S(1)} %get-tuple-element.26), channel_id=1, source_target_pairs={{4,0},{8,4},{12,8},{16,12},{20,16},{24,20},{28,24},{0,28},{5,1},{9... | collective-permute-start | bytes 6152 | tf_op jit(solution)/shard_map/ppermute | solution.py:23
  43.6 4.8 %collective-permute-done.5 = f32[4,8,16,1]{3,2,1,0:T(8,128)S(1)} collective-permute-done((f32[4,8,16,1]{3,2,1,0:T(8,128)S(1)}, f32[4,8,16,1]{3,2,1,0:T(8,128)S(1)}, u32[]{:S(2)}, u32[]{:S(2)}) %collective-permute-start.5) | collective-permute-done | bytes 2080 | tf_op jit(solution)/shard_map/ppermute | solution.py:23
  48.4 5.9 %collective-permute-done.4 = f32[4,8,16,1]{3,2,1,0:T(8,128)S(1)} collective-permute-done((f32[4,8,16,1]{3,2,1,0:T(8,128)S(1)}, f32[4,8,16,1]{3,2,1,0:T(8,128)S(1)}, u32[]{:S(2)}, u32[]{:S(2)}) %collective-permute-start.4) | collective-permute-done | bytes 2080 | tf_op jit(solution)/shard_map/ppermute | solution.py:22
  54.6 1.3 collective-permute-start.7
  55.9 3.5 %collective-permute-start.6 = (f32[4,8,1,130]{3,2,1,0:T(1,128)S(1)}, f32[4,8,1,130]{3,2,1,0:T(1,128)S(1)}, u32[]{:S(2)}, u32[]{:S(2)}) collective-permute-start(f32[4,8,1,130]{3,2,1,0:T(1,128)S(1)} %get-tuple-element.17), channel_id=1, source_target_pairs={{0,1},{1,2},{2,3},{4,5},{5,6},{6,7},{8,9},{9,10},{10,11},{12,13},{... | collective-permute-start | bytes 49928 | tf_op jit(solution)/shard_map/ppermute | solution.py:22
  59.5 0.8 collective-permute-done.6
  60.2 0.4 pad_maximum_fusion.11
  60.7 0.6 subtract_multiply_fusion
  62.3 1.1 fusion.36
  63.7 73.0 %all-reduce.6.cloned.1.call-done = f32[512,128]{1,0:T(8,128)} async-done(((f32[512,128]{1,0:T(8,128)}), f32[512,128]{1,0:T(8,128)}) %all-reduce.6.cloned.1.call-update) | async-done | bytes 262160 | tf_op jit(solution)/shard_map/psum | solution.py:108
  136.7 1.4 fusion.14
  138.1 0.7 multiply_add_fusion
  (51 shorter events, 3.5 us)
Async XLA Ops:
  6.5 130.2 %all-reduce.6.cloned.1.call-start = ((), (), s32[]{:S(2)}) async-start(), calls=%async_computation | async-start | bytes 524288 | tf_op jit(solution)/shard_map/psum | solution.py:108
  7.4 7.7 %copy-start.3 = (s32[16]{0:T(128)S(1)}, s32[16]{0:T(128)}, u32[]{:S(2)}) copy-start(s32[16]{0:T(128)} %param.9) | copy-start | bytes 196
  7.4 7.8 %copy-start.2 = (s32[8,16,128]{2,1,0:T(8,128)S(1)}, s32[8,16,128]{2,1,0:T(8,128)}, u32[]{:S(2)}) copy-start(s32[8,16,128]{2,1,0:T(8,128)} %param.7) | copy-start | bytes 196612
  7.4 22.0 %copy-start = (f32[4,8,16,128]{3,2,1,0:T(8,128)S(1)}, f32[4,8,16,128]{3,2,1,0:T(8,128)}, u32[]{:S(2)}) copy-start(f32[4,8,16,128]{3,2,1,0:T(8,128)} %param.5) | copy-start | bytes 786436
  7.4 22.0 %copy-start.1 = (f32[8,16,128]{2,1,0:T(8,128)S(1)}, f32[8,16,128]{2,1,0:T(8,128)}, u32[]{:S(2)}) copy-start(f32[8,16,128]{2,1,0:T(8,128)} %param.6) | copy-start | bytes 196612
  8.7 20.6 %collective-permute-start.1 = (f32[6,8,16,1]{3,2,1,0:T(8,128)S(1)}, f32[6,8,16,1]{3,2,1,0:T(8,128)S(1)}, u32[]{:S(2)}, u32[]{:S(2)}) collective-permute-start(f32[6,8,16,1]{3,2,1,0:T(8,128)S(1)} %get-tuple-element.24), channel_id=1, source_target_pairs={{4,0},{8,4},{12,8},{16,12},{20,16},{24,20},{28,24},{0,28},{5,1},{9... | collective-permute-start | bytes 9224 | tf_op jit(solution)/shard_map/ppermute | solution.py:23
  14.7 14.7 %collective-permute-start = (f32[6,8,16,1]{3,2,1,0:T(8,128)S(1)}, f32[6,8,16,1]{3,2,1,0:T(8,128)S(1)}, u32[]{:S(2)}, u32[]{:S(2)}) collective-permute-start(f32[6,8,16,1]{3,2,1,0:T(8,128)S(1)} %get-tuple-element.23), channel_id=1, source_target_pairs={{0,4},{4,8},{8,12},{12,16},{16,20},{20,24},{24,28},{28,0},{1,5},{5... | collective-permute-start | bytes 9224 | tf_op jit(solution)/shard_map/ppermute | solution.py:22
  29.8 3.4 %collective-permute-start.2 = (f32[6,8,1,130]{3,2,1,0:T(1,128)S(1)}, f32[6,8,1,130]{3,2,1,0:T(1,128)S(1)}, u32[]{:S(2)}, u32[]{:S(2)}) collective-permute-start(f32[6,8,1,130]{3,2,1,0:T(1,128)S(1)} %get-tuple-element.10), channel_id=1, source_target_pairs={{0,1},{1,2},{2,3},{4,5},{5,6},{6,7},{8,9},{9,10},{10,11},{12,13},{... | collective-permute-start | bytes 74888 | tf_op jit(solution)/shard_map/ppermute | solution.py:22
  31.7 4.3 %collective-permute-start.3 = (f32[6,8,1,130]{3,2,1,0:T(1,128)S(1)}, f32[6,8,1,130]{3,2,1,0:T(1,128)S(1)}, u32[]{:S(2)}, u32[]{:S(2)}) collective-permute-start(f32[6,8,1,130]{3,2,1,0:T(1,128)S(1)} %get-tuple-element.9), channel_id=1, source_target_pairs={{1,0},{2,1},{3,2},{5,4},{6,5},{7,6},{9,8},{10,9},{11,10},{13,12},{... | collective-permute-start | bytes 74888 | tf_op jit(solution)/shard_map/ppermute | solution.py:23
  38.8 9.6 %collective-permute-start.5 = (f32[4,8,16,1]{3,2,1,0:T(8,128)S(1)}, f32[4,8,16,1]{3,2,1,0:T(8,128)S(1)}, u32[]{:S(2)}, u32[]{:S(2)}) collective-permute-start(f32[4,8,16,1]{3,2,1,0:T(8,128)S(1)} %get-tuple-element.26), channel_id=1, source_target_pairs={{4,0},{8,4},{12,8},{16,12},{20,16},{24,20},{28,24},{0,28},{5,1},{9... | collective-permute-start | bytes 6152 | tf_op jit(solution)/shard_map/ppermute | solution.py:23
  43.6 10.8 %collective-permute-start.4 = (f32[4,8,16,1]{3,2,1,0:T(8,128)S(1)}, f32[4,8,16,1]{3,2,1,0:T(8,128)S(1)}, u32[]{:S(2)}, u32[]{:S(2)}) collective-permute-start(f32[4,8,16,1]{3,2,1,0:T(8,128)S(1)} %get-tuple-element.25), channel_id=1, source_target_pairs={{0,4},{4,8},{8,12},{12,16},{16,20},{20,24},{24,28},{28,0},{1,5},{5... | collective-permute-start | bytes 6152 | tf_op jit(solution)/shard_map/ppermute | solution.py:22
  54.6 4.8 %collective-permute-start.7 = (f32[4,8,1,130]{3,2,1,0:T(1,128)S(1)}, f32[4,8,1,130]{3,2,1,0:T(1,128)S(1)}, u32[]{:S(2)}, u32[]{:S(2)}) collective-permute-start(f32[4,8,1,130]{3,2,1,0:T(1,128)S(1)} %get-tuple-element.18), channel_id=1, source_target_pairs={{1,0},{2,1},{3,2},{5,4},{6,5},{7,6},{9,8},{10,9},{11,10},{13,12},{... | collective-permute-start | bytes 49928 | tf_op jit(solution)/shard_map/ppermute | solution.py:23
  55.9 4.3 %collective-permute-start.6 = (f32[4,8,1,130]{3,2,1,0:T(1,128)S(1)}, f32[4,8,1,130]{3,2,1,0:T(1,128)S(1)}, u32[]{:S(2)}, u32[]{:S(2)}) collective-permute-start(f32[4,8,1,130]{3,2,1,0:T(1,128)S(1)} %get-tuple-element.17), channel_id=1, source_target_pairs={{0,1},{1,2},{2,3},{4,5},{5,6},{6,7},{8,9},{9,10},{10,11},{12,13},{... | collective-permute-start | bytes 49928 | tf_op jit(solution)/shard_map/ppermute | solution.py:22
  62.0 1.5 copy-start.4
Sparse Core Ops, SparseCore 0:
  63.6 73.0 all-reduce.5
where the time goes:
time: 146 us
  waiting for transfers between devices  101 us (69%)
  starting transfers between devices  18.9 us (13%)
  between operations  13.7 us (9%)
  other arithmetic  7.99 us (5%)
  matrix products  2.53 us (2%)
    psum x1, waiting for transfers between devices, shards(): totals = lax.psum(partial_sum, 'lon')  73 us
    ppermute x4, waiting for transfers between devices, with_halo(): after = lax.ppermute(leading, axis, down)  21.6 us
    ppermute x4, starting transfers between devices, with_halo(): after = lax.ppermute(leading, axis, down)  13.5 us
    ppermute x4, waiting for transfers between devices, with_halo(): before = lax.ppermute(last, axis, up)  6.89 us
    ppermute x4, starting transfers between devices, with_halo(): before = lax.ppermute(last, axis, up)  5.41 us
  transfers between devices with their start and end apart: 9, of which 7 were waited for; matrix products, arithmetic and copies ran while one was open for 1% of the time, Pallas kernels for 0%

commit v1 on v0

--- a/solution.py
+++ b/solution.py
@@ -10,6 +10,15 @@
 diffusion = 0.05
 vertical_mix = 0.5
 time_step = 0.05
+
+
+def sum_by_hops(value, mesh_axis):
+    count = lax.axis_size(mesh_axis)
+    total, far = (value, 1)
+    while far < count:
+        total = total + lax.ppermute(total, mesh_axis, [(i, i ^ far) for i in range(count)])
+        far = 2 * far
+    return total
 
 
 def with_halo(array, sides, width, wrap):
@@ -105,7 +114,7 @@
     partial_sum = jnp.dot(
         flat, basis, precision=lax.Precision.HIGHEST, preferred_element_type=jnp.float32
     )
-    totals = lax.psum(partial_sum, "lon")
+    totals = sum_by_hops(partial_sum, "lon")
     smooth = jnp.dot(
         totals * mode_weights(row_counts, MAXM, nlon),
         basis.T,

time: 146 us -> 89.7 us (0.61)
  waiting for transfers between devices: 101 us -> 57.4 us
  between operations: 13.7 us -> 0.3 us
  starting transfers between devices: 18.9 us -> 21.7 us
  matrix products: 2.53 us -> 0.9 us
    psum x1 -> x0, waiting for transfers between devices: 73 us -> none  [shards(): totals = lax.psum(partial_sum, 'lon')]
    ppermute x0 -> x3, waiting for transfers between devices: none -> 28.8 us  [sum_by_hops(): lax.ppermute(total, mesh_axis, [(i, i ^ far) for i in range(count)])]
    ppermute x0 -> x3, starting transfers between devices: none -> 2.81 us  [sum_by_hops(): lax.ppermute(total, mesh_axis, [(i, i ^ far) for i in range(count)])]
  transfers between devices with their start and end apart: 9 -> 11, of which waited for: 7 -> 9; matrix products, arithmetic and copies ran while one was open for 1% -> 1% of each run, Pallas kernels for 0% -> 0%
where the time goes in v1:
time: 89.7 us; the launch traced here: 89.4 us
  waiting for transfers between devices  57.4 us (64%)
  starting transfers between devices  21.7 us (24%)
  other arithmetic  8.05 us (9%)
  local copies, waits for them, and re-layouts  1.09 us (1%)
  matrix products  0.9 us (1%)
    ppermute x3, waiting for transfers between devices, sum_by_hops(): lax.ppermute(total, mesh_axis, [(i, i ^ far) for i in range(count)])  28.8 us
    ppermute x4, waiting for transfers between devices, with_halo(): after = lax.ppermute(leading, axis, down)  21.7 us
    ppermute x4, starting transfers between devices, with_halo(): after = lax.ppermute(leading, axis, down)  13.5 us
    ppermute x4, waiting for transfers between devices, with_halo(): before = lax.ppermute(last, axis, up)  6.89 us
    ppermute x4, starting transfers between devices, with_halo(): before = lax.ppermute(last, axis, up)  5.41 us
    ppermute x3, starting transfers between devices, sum_by_hops(): lax.ppermute(total, mesh_axis, [(i, i ^ far) for i in range(count)])  2.81 us
  transfers between devices with their start and end apart: 11, of which 9 were waited for; matrix products, arithmetic and copies ran while one was open for 1% of the time, Pallas kernels for 0%

profile of v1, /device:TPU:0, one launch (start us, length us, event | category | flops | bytes accessed | tf_op | source)
XLA Modules:
  0.0 89.4 jit_solution(8609111933586692719)
XLA Ops:
  0.0 0.8 convert_bitcast_fusion
  0.9 1.1 %pad_maximum_fusion.13 = f32[6,8,16,128]{3,2,1,0:T(8,128)S(1)} fusion(f32[1,8,16,128]{3,2,1,0:T(8,128)S(1)} %convert_bitcast_fusion, f32[1,8,16,128]{3,2,1,0:T(8,128)} %bitcast.19, f32[4,8,16,128]{3,2,1,0:T(8,128)} %param.5), kind=kLoop, calls=%fused_computation.18 | loop fusion | flops 196608 | bytes 786432 | tf_op jit(solution)/shard_map/concatenate | solution.py:96
  2.1 6.1 %collective-permute-start.1 = (f32[6,8,16,1]{3,2,1,0:T(8,128)S(1)}, f32[6,8,16,1]{3,2,1,0:T(8,128)S(1)}, u32[]{:S(2)}, u32[]{:S(2)}) collective-permute-start(f32[6,8,16,1]{3,2,1,0:T(8,128)S(1)} %get-tuple-element.24), channel_id=1, source_target_pairs={{4,0},{8,4},{12,8},{16,12},{20,16},{24,20},{28,24},{0,28},{5,1},{9... | collective-permute-start | bytes 9224 | tf_op jit(solution)/shard_map/ppermute | solution.py:32
  8.3 14.3 %collective-permute-done.1 = f32[6,8,16,1]{3,2,1,0:T(8,128)S(1)} collective-permute-done((f32[6,8,16,1]{3,2,1,0:T(8,128)S(1)}, f32[6,8,16,1]{3,2,1,0:T(8,128)S(1)}, u32[]{:S(2)}, u32[]{:S(2)}) %collective-permute-start.1) | collective-permute-done | bytes 3104 | tf_op jit(solution)/shard_map/ppermute | solution.py:32
  23.2 1.9 %collective-permute-start.2 = (f32[6,8,1,130]{3,2,1,0:T(1,128)S(1)}, f32[6,8,1,130]{3,2,1,0:T(1,128)S(1)}, u32[]{:S(2)}, u32[]{:S(2)}) collective-permute-start(f32[6,8,1,130]{3,2,1,0:T(1,128)S(1)} %get-tuple-element.10), channel_id=1, source_target_pairs={{0,1},{1,2},{2,3},{4,5},{5,6},{6,7},{8,9},{9,10},{10,11},{12,13},{... | collective-permute-start | bytes 74888 | tf_op jit(solution)/shard_map/ppermute | solution.py:31
  25.1 1.3 %collective-permute-start.3 = (f32[6,8,1,130]{3,2,1,0:T(1,128)S(1)}, f32[6,8,1,130]{3,2,1,0:T(1,128)S(1)}, u32[]{:S(2)}, u32[]{:S(2)}) collective-permute-start(f32[6,8,1,130]{3,2,1,0:T(1,128)S(1)} %get-tuple-element.9), channel_id=1, source_target_pairs={{1,0},{2,1},{3,2},{5,4},{6,5},{7,6},{9,8},{10,9},{11,10},{13,12},{... | collective-permute-start | bytes 74888 | tf_op jit(solution)/shard_map/ppermute | solution.py:32
  26.5 2.9 %collective-permute-done.3 = f32[6,8,1,130]{3,2,1,0:T(1,128)S(1)} collective-permute-done((f32[6,8,1,130]{3,2,1,0:T(1,128)S(1)}, f32[6,8,1,130]{3,2,1,0:T(1,128)S(1)}, u32[]{:S(2)}, u32[]{:S(2)}) %collective-permute-start.3) | collective-permute-done | bytes 24992 | tf_op jit(solution)/shard_map/ppermute | solution.py:32
  29.4 0.5 pad_maximum_fusion
  30.2 0.6 subtract_multiply_fusion.2
  32.2 4.8 %collective-permute-start.5 = (f32[4,8,16,1]{3,2,1,0:T(8,128)S(1)}, f32[4,8,16,1]{3,2,1,0:T(8,128)S(1)}, u32[]{:S(2)}, u32[]{:S(2)}) collective-permute-start(f32[4,8,16,1]{3,2,1,0:T(8,128)S(1)} %get-tuple-element.26), channel_id=1, source_target_pairs={{4,0},{8,4},{12,8},{16,12},{20,16},{24,20},{28,24},{0,28},{5,1},{9... | collective-permute-start | bytes 6152 | tf_op jit(solution)/shard_map/ppermute | solution.py:32
  37.4 4.5 %collective-permute-done.5 = f32[4,8,16,1]{3,2,1,0:T(8,128)S(1)} collective-permute-done((f32[4,8,16,1]{3,2,1,0:T(8,128)S(1)}, f32[4,8,16,1]{3,2,1,0:T(8,128)S(1)}, u32[]{:S(2)}, u32[]{:S(2)}) %collective-permute-start.5) | collective-permute-done | bytes 2080 | tf_op jit(solution)/shard_map/ppermute | solution.py:32
  41.9 5.9 %collective-permute-done.4 = f32[4,8,16,1]{3,2,1,0:T(8,128)S(1)} collective-permute-done((f32[4,8,16,1]{3,2,1,0:T(8,128)S(1)}, f32[4,8,16,1]{3,2,1,0:T(8,128)S(1)}, u32[]{:S(2)}, u32[]{:S(2)}) %collective-permute-start.4) | collective-permute-done | bytes 2080 | tf_op jit(solution)/shard_map/ppermute | solution.py:31
  48.1 1.3 %collective-permute-start.7 = (f32[4,8,1,130]{3,2,1,0:T(1,128)S(1)}, f32[4,8,1,130]{3,2,1,0:T(1,128)S(1)}, u32[]{:S(2)}, u32[]{:S(2)}) collective-permute-start(f32[4,8,1,130]{3,2,1,0:T(1,128)S(1)} %get-tuple-element.18), channel_id=1, source_target_pairs={{1,0},{2,1},{3,2},{5,4},{6,5},{7,6},{9,8},{10,9},{11,10},{13,12},{... | collective-permute-start | bytes 49928 | tf_op jit(solution)/shard_map/ppermute | solution.py:32
  49.4 3.5 %collective-permute-start.6 = (f32[4,8,1,130]{3,2,1,0:T(1,128)S(1)}, f32[4,8,1,130]{3,2,1,0:T(1,128)S(1)}, u32[]{:S(2)}, u32[]{:S(2)}) collective-permute-start(f32[4,8,1,130]{3,2,1,0:T(1,128)S(1)} %get-tuple-element.17), channel_id=1, source_target_pairs={{0,1},{1,2},{2,3},{4,5},{5,6},{6,7},{8,9},{9,10},{10,11},{12,13},{... | collective-permute-start | bytes 49928 | tf_op jit(solution)/shard_map/ppermute | solution.py:31
  52.9 0.8 collective-permute-done.6
  54.1 0.6 subtract_multiply_fusion
  55.7 0.4 fusion.37
  56.2 2.1 %collective-permute-start.8 = (f32[512,128]{1,0:T(8,128)S(1)}, f32[512,128]{1,0:T(8,128)S(1)}, u32[]{:S(2)}, u32[]{:S(2)}) collective-permute-start(f32[512,128]{1,0:T(8,128)S(1)} %fusion.37), channel_id=1, source_target_pairs={{0,4},{4,0},{8,12},{12,8},{16,20},{20,16},{24,28},{28,24},{1,5},{5... | collective-permute-start | bytes 786440 | tf_op jit(solution)/shard_map/ppermute | solution.py:19
  58.3 6.3 %collective-permute-done.8 = f32[512,128]{1,0:T(8,128)S(1)} collective-permute-done((f32[512,128]{1,0:T(8,128)S(1)}, f32[512,128]{1,0:T(8,128)S(1)}, u32[]{:S(2)}, u32[]{:S(2)}) %collective-permute-start.8) | collective-permute-done | bytes 262176 | tf_op jit(solution)/shard_map/ppermute | solution.py:19
  64.8 8.8 %collective-permute-done.9 = f32[512,128]{1,0:T(8,128)S(1)} collective-permute-done((f32[512,128]{1,0:T(8,128)S(1)}, f32[512,128]{1,0:T(8,128)S(1)}, u32[]{:S(2)}, u32[]{:S(2)}) %collective-permute-start.9) | collective-permute-done | bytes 262176 | tf_op jit(solution)/shard_map/ppermute | solution.py:19
  73.6 0.6 collective-permute-start.10
  74.5 13.7 %collective-permute-done.10 = f32[512,128]{1,0:T(8,128)S(1)} collective-permute-done((f32[512,128]{1,0:T(8,128)S(1)}, f32[512,128]{1,0:T(8,128)S(1)}, u32[]{:S(2)}, u32[]{:S(2)}) %collective-permute-start.10) | collective-permute-done | bytes 262176 | tf_op jit(solution)/shard_map/ppermute | solution.py:19
  88.2 0.5 fusion.14
  88.7 0.7 multiply_add_fusion
  (56 shorter events, 5.0 us)
Async XLA Ops:
  0.8 22.0 %copy-start = (f32[4,8,16,128]{3,2,1,0:T(8,128)S(1)}, f32[4,8,16,128]{3,2,1,0:T(8,128)}, u32[]{:S(2)}) copy-start(f32[4,8,16,128]{3,2,1,0:T(8,128)} %param.5) | copy-start | bytes 786436
  0.8 22.0 %copy-start.1 = (f32[8,16,128]{2,1,0:T(8,128)S(1)}, f32[8,16,128]{2,1,0:T(8,128)}, u32[]{:S(2)}) copy-start(f32[8,16,128]{2,1,0:T(8,128)} %param.6) | copy-start | bytes 196612
  2.1 20.6 %collective-permute-start.1 = (f32[6,8,16,1]{3,2,1,0:T(8,128)S(1)}, f32[6,8,16,1]{3,2,1,0:T(8,128)S(1)}, u32[]{:S(2)}, u32[]{:S(2)}) collective-permute-start(f32[6,8,16,1]{3,2,1,0:T(8,128)S(1)} %get-tuple-element.24), channel_id=1, source_target_pairs={{4,0},{8,4},{12,8},{16,12},{20,16},{24,20},{28,24},{0,28},{5,1},{9... | collective-permute-start | bytes 9224 | tf_op jit(solution)/shard_map/ppermute | solution.py:32
  8.2 14.7 %collective-permute-start = (f32[6,8,16,1]{3,2,1,0:T(8,128)S(1)}, f32[6,8,16,1]{3,2,1,0:T(8,128)S(1)}, u32[]{:S(2)}, u32[]{:S(2)}) collective-permute-start(f32[6,8,16,1]{3,2,1,0:T(8,128)S(1)} %get-tuple-element.23), channel_id=1, source_target_pairs={{0,4},{4,8},{8,12},{12,16},{16,20},{20,24},{24,28},{28,0},{1,5},{5... | collective-permute-start | bytes 9224 | tf_op jit(solution)/shard_map/ppermute | solution.py:31
  23.2 3.3 %collective-permute-start.2 = (f32[6,8,1,130]{3,2,1,0:T(1,128)S(1)}, f32[6,8,1,130]{3,2,1,0:T(1,128)S(1)}, u32[]{:S(2)}, u32[]{:S(2)}) collective-permute-start(f32[6,8,1,130]{3,2,1,0:T(1,128)S(1)} %get-tuple-element.10), channel_id=1, source_target_pairs={{0,1},{1,2},{2,3},{4,5},{5,6},{6,7},{8,9},{9,10},{10,11},{12,13},{... | collective-permute-start | bytes 74888 | tf_op jit(solution)/shard_map/ppermute | solution.py:31
  25.1 4.3 %collective-permute-start.3 = (f32[6,8,1,130]{3,2,1,0:T(1,128)S(1)}, f32[6,8,1,130]{3,2,1,0:T(1,128)S(1)}, u32[]{:S(2)}, u32[]{:S(2)}) collective-permute-start(f32[6,8,1,130]{3,2,1,0:T(1,128)S(1)} %get-tuple-element.9), channel_id=1, source_target_pairs={{1,0},{2,1},{3,2},{5,4},{6,5},{7,6},{9,8},{10,9},{11,10},{13,12},{... | collective-permute-start | bytes 74888 | tf_op jit(solution)/shard_map/ppermute | solution.py:32
  32.2 9.6 %collective-permute-start.5 = (f32[4,8,16,1]{3,2,1,0:T(8,128)S(1)}, f32[4,8,16,1]{3,2,1,0:T(8,128)S(1)}, u32[]{:S(2)}, u32[]{:S(2)}) collective-permute-start(f32[4,8,16,1]{3,2,1,0:T(8,128)S(1)} %get-tuple-element.26), channel_id=1, source_target_pairs={{4,0},{8,4},{12,8},{16,12},{20,16},{24,20},{28,24},{0,28},{5,1},{9... | collective-permute-start | bytes 6152 | tf_op jit(solution)/shard_map/ppermute | solution.py:32
  37.0 10.8 %collective-permute-start.4 = (f32[4,8,16,1]{3,2,1,0:T(8,128)S(1)}, f32[4,8,16,1]{3,2,1,0:T(8,128)S(1)}, u32[]{:S(2)}, u32[]{:S(2)}) collective-permute-start(f32[4,8,16,1]{3,2,1,0:T(8,128)S(1)} %get-tuple-element.25), channel_id=1, source_target_pairs={{0,4},{4,8},{8,12},{12,16},{16,20},{20,24},{24,28},{28,0},{1,5},{5... | collective-permute-start | bytes 6152 | tf_op jit(solution)/shard_map/ppermute | solution.py:31
  48.1 4.8 %collective-permute-start.7 = (f32[4,8,1,130]{3,2,1,0:T(1,128)S(1)}, f32[4,8,1,130]{3,2,1,0:T(1,128)S(1)}, u32[]{:S(2)}, u32[]{:S(2)}) collective-permute-start(f32[4,8,1,130]{3,2,1,0:T(1,128)S(1)} %get-tuple-element.18), channel_id=1, source_target_pairs={{1,0},{2,1},{3,2},{5,4},{6,5},{7,6},{9,8},{10,9},{11,10},{13,12},{... | collective-permute-start | bytes 49928 | tf_op jit(solution)/shard_map/ppermute | solution.py:32
  49.4 4.3 %collective-permute-start.6 = (f32[4,8,1,130]{3,2,1,0:T(1,128)S(1)}, f32[4,8,1,130]{3,2,1,0:T(1,128)S(1)}, u32[]{:S(2)}, u32[]{:S(2)}) collective-permute-start(f32[4,8,1,130]{3,2,1,0:T(1,128)S(1)} %get-tuple-element.17), channel_id=1, source_target_pairs={{0,1},{1,2},{2,3},{4,5},{5,6},{6,7},{8,9},{9,10},{10,11},{12,13},{... | collective-permute-start | bytes 49928 | tf_op jit(solution)/shard_map/ppermute | solution.py:31
  55.7 9.0 %copy-start.3 = (s32[16]{0:T(128)S(1)}, s32[16]{0:T(128)}, u32[]{:S(2)}) copy-start(s32[16]{0:T(128)} %param.9) | copy-start | bytes 196
  55.7 9.0 %copy-start.2 = (s32[8,16,128]{2,1,0:T(8,128)S(1)}, s32[8,16,128]{2,1,0:T(8,128)}, u32[]{:S(2)}) copy-start(s32[8,16,128]{2,1,0:T(8,128)} %param.7) | copy-start | bytes 196612
  55.7 18.5 %copy-start.4 = (s32[16]{0:T(128)S(1)}, s32[16]{0:T(128)}, u32[]{:S(2)}) copy-start(s32[16]{0:T(128)} %param.8) | copy-start | bytes 196
  56.2 8.4 %collective-permute-start.8 = (f32[512,128]{1,0:T(8,128)S(1)}, f32[512,128]{1,0:T(8,128)S(1)}, u32[]{:S(2)}, u32[]{:S(2)}) collective-permute-start(f32[512,128]{1,0:T(8,128)S(1)} %fusion.37), channel_id=1, source_target_pairs={{0,4},{4,0},{8,12},{12,8},{16,20},{20,16},{24,28},{28,24},{1,5},{5... | collective-permute-start | bytes 786440 | tf_op jit(solution)/shard_map/ppermute | solution.py:19
  64.6 9.0 %collective-permute-start.9 = (f32[512,128]{1,0:T(8,128)S(1)}, f32[512,128]{1,0:T(8,128)S(1)}, u32[]{:S(2)}, u32[]{:S(2)}) collective-permute-start(f32[512,128]{1,0:T(8,128)S(1)} %add.125), channel_id=1, source_target_pairs={{0,8},{4,12},{8,0},{12,4},{16,24},{20,28},{24,16},{28,20},{1,9},{5... | collective-permute-start | bytes 786440 | tf_op jit(solution)/shard_map/ppermute | solution.py:19
  73.6 14.6 %collective-permute-start.10 = (f32[512,128]{1,0:T(8,128)S(1)}, f32[512,128]{1,0:T(8,128)S(1)}, u32[]{:S(2)}, u32[]{:S(2)}) collective-permute-start(f32[512,128]{1,0:T(8,128)S(1)} %add.126), channel_id=1, source_target_pairs={{0,16},{4,20},{8,24},{12,28},{16,0},{20,4},{24,8},{28,12},{1,17},{... | collective-permute-start | bytes 786440 | tf_op jit(solution)/shard_map/ppermute | solution.py:19
